TPU v7x, 32 devices: a whole 2x2x4 slice. The times are simulated.
32 devices in a mesh: seg: 8 (over y, x, core), head: 4 (over z).
Axes of the slice: x: 2, y: 2, z: 4, core: 2. Of those that a mesh axis runs over, the one named last changes fastest.
Arguments:
- layer_input: bfloat16 [1, 4096, 2048], P(None, 'seg', 'head'), may hold values from -160 to 160, as said below
- w_qkv: bfloat16 [2048, 3, 1024], P(None, None, 'head'), may hold values from -3 to 3
- comp_weight: bfloat16 [3, 2, 1024], P(None, None, 'head'), may hold values from -2.5 to 2.5
- w_out: bfloat16 [1024, 2048], P('seg', 'head'), may hold values from -1.5 to 1.5
Outputs:
- attn_out: bfloat16 [1, 4096, 2048], P(None, 'seg', 'head')
Inputs may be any that keep to these rules, and one draw needn't show every extreme that they name: layer_input varies in scale from feature to feature and from token to token.
All inputs are finite; a program needn't handle non-finite values.
Results may differ from a plain program's by a relative error of at most 0.0089.
Values may be sent and summed in bfloat16 or wider, within the bound.
No kernel may reach another device: no remote copies, remote signals or barrier semaphores. Data moves between devices by JAX's collectives and lax.ppermute only.
A program may use at most 64 MiB of HBM per device.

v0:
```python
import math
import jax
import jax.numpy as jnp
from jax import lax
from jax.sharding import PartitionSpec as P

DH = 128


def passed_along(block, axis, distance):
    devices = range(lax.axis_size(axis))
    route = [(i - distance, i) for i in devices if i - distance in devices]
    return lax.ppermute(block, axis, route)


def layer_norm(values):
    center_mean = jnp.mean(values, axis=-1, keepdims=True)
    centered = values - center_mean
    variance = jnp.mean(centered * centered, axis=-1, keepdims=True)
    return centered * lax.rsqrt(variance + 1e-05)


def compress_block(source, weight):
    batch, pair, length, width = source.shape
    grouped = source.reshape(batch, pair, length // 3, 3, width)
    mixed = jnp.einsum("bkltc,tkc->bklc", grouped, weight, preferred_element_type=jnp.float32)
    return mixed.astype(jnp.bfloat16)


def key_allowed(seg_len, segment):
    query_pos = jnp.arange(seg_len)[:, None]
    key_pos = jnp.arange(3 * seg_len)[None, :]
    own_part = (key_pos >= 2 * seg_len) & (key_pos - 2 * seg_len <= query_pos)
    memory_part = (key_pos >= seg_len) & (key_pos < 2 * seg_len) & (segment >= 1)
    comp_part = (key_pos < seg_len) & (segment >= 4)
    return own_part | memory_part | comp_part


def attend(queries, key_vals, segment):
    batch, seg_len, width = queries.shape
    heads_here = width // DH
    query_heads = queries.reshape(batch, seg_len, heads_here, DH)
    key_heads = key_vals[:, 0].reshape(batch, 3 * seg_len, heads_here, DH)
    value_heads = key_vals[:, 1].reshape(batch, 3 * seg_len, heads_here, DH)
    scores = jnp.einsum(
        "bqhd,bkhd->bhqk", query_heads, key_heads, preferred_element_type=jnp.float32
    )
    scores = scores / math.sqrt(DH)
    allowed = key_allowed(seg_len, segment)
    scores = jnp.where(allowed[None, None], scores, jnp.float32(-1e30))
    highest = jnp.max(scores, axis=-1, keepdims=True)
    exponent = jnp.exp(scores - highest)
    weights = (exponent / jnp.sum(exponent, axis=-1, keepdims=True)).astype(jnp.bfloat16)
    mixed = jnp.einsum("bhqk,bkhd->bqhd", weights, value_heads, preferred_element_type=jnp.float32)
    return mixed.astype(jnp.bfloat16).reshape(batch, seg_len, width)


def local(layer_input, w_qkv, comp_weight, w_out):
    gathered = lax.all_gather(layer_input, "head", axis=2, tiled=True)
    normed = layer_norm(gathered.astype(jnp.float32)).astype(jnp.bfloat16)
    projected = jnp.einsum("bld,dkc->bklc", normed, w_qkv, preferred_element_type=jnp.float32)
    projected = projected.astype(jnp.bfloat16)
    queries = projected[:, 0]
    key_vals = projected[:, 1:3]
    memory = passed_along(key_vals, "seg", 1)
    second_back = passed_along(memory, "seg", 1)
    upcoming = compress_block(jnp.concatenate([second_back, memory, key_vals], axis=2), comp_weight)
    compressed = passed_along(upcoming, "seg", 2)
    segment = lax.axis_index("seg")
    joined = jnp.concatenate([compressed, memory, key_vals], axis=2)
    context = attend(queries, joined, segment)
    full_ctx = lax.all_gather(context, "head", axis=2, tiled=True)
    whole_out = lax.all_gather(w_out, "seg", axis=0, tiled=True)
    result_sum = jnp.einsum("blr,rc->blc", full_ctx, whole_out, preferred_element_type=jnp.float32)
    return result_sum.astype(jnp.bfloat16)


def solution(mesh):
    return jax.shard_map(
        local,
        mesh=mesh,
        in_specs=(
            P(None, "seg", "head"),
            P(None, None, "head"),
            P(None, None, "head"),
            P("seg", "head"),
        ),
        out_specs=P(None, "seg", "head"),
        check_vma=False,
    )
```

profile of v0, /device:TPU:0, one launch (start us, length us, event | category | flops | bytes accessed | tf_op | source)
XLA Modules:
  0.0 164.3 jit_solution(6512609901003673193)
XLA Ops:
  7.4 0.7 all-gather.4.cloned.1.call-update
  8.1 0.0 all-gather.8.cloned.1.call-start
  8.1 50.0 %all-gather.4.cloned.1.call-done = bf16[1,512,2048]{2,1,0:T(8,128)(2,1)} async-done(((bf16[1,512,512]{2,1,0:T(8,128)(2,1)}), bf16[1,512,2048]{2,1,0:T(8,128)(2,1)}) %all-gather.4.cloned.1.call-update) | async-done | bytes 2097168 | tf_op jit(solution)/shard_map/all_gather | solution.py:59
  58.2 2.1 %convert_reduce_fusion = f32[512]{0:T(512)S(1)} fusion(bf16[1,512,2048]{2,1,0:T(8,128)(2,1)} %all-gather.4.cloned.1.call-done), kind=kLoop, calls=%fused_computation.6 | loop fusion | flops 2096640 | bytes 2099200 | tf_op jit(solution)/shard_map/reduce_sum | solution.py:17
  60.3 0.1 copy-done.1
  60.4 0.7 fusion.4
  61.1 0.0 copy-start.4
  61.1 2.0 %fusion.21 = bf16[1,3,512,256]{2,3,1,0:T(8,128)(2,1)S(1)} fusion(bf16[2048,3,256]{2,0,1:T(8,128)(2,1)S(1)} %copy-done, bf16[1,512,2048]{2,1,0:T(8,128)(2,1)S(1)} %copy-done.1, f32[512]{0:T(512)S(1)} %add_rsqrt_fusion, f32[512]{0:T(512)S(1)} %broadcast_multiply_fusion), kind=kOutput, calls=%fused_computation.29 | convolution fusion | flops 1615200256 | bytes 6033408 | tf_op jit(solution)/shard_map/bld,dkc->bklc/dot_general | solution.py:61
  63.1 0.0 copy-start.2
  63.1 0.8 copy-done.2
  64.0 2.4 %collective-permute-start = (bf16[1,2,512,256]{2,3,1,0:T(8,128)(2,1)S(1)}, bf16[1,2,512,256]{2,3,1,0:T(8,128)(2,1)}, u32[]{:S(2)}, u32[]{:S(2)}) collective-permute-start(bf16[1,2,512,256]{2,3,1,0:T(8,128)(2,1)S(1)} %slice.16), channel_id=1, source_target_pairs={{0,4},{4,8},{8,12},{12,16},{16,20},{20,24},{24,28},{1,5},{5,9},{9,... | collective-permute-start | bytes 1572872 | tf_op jit(solution)/shard_map/ppermute | solution.py:13
  66.4 0.8 collective-permute-done
  67.2 9.1 %collective-permute-start.1 = (bf16[1,2,512,256]{2,3,1,0:T(8,128)(2,1)}, bf16[1,2,512,256]{2,3,1,0:T(8,128)(2,1)}, u32[]{:S(2)}, u32[]{:S(2)}) collective-permute-start(bf16[1,2,512,256]{2,3,1,0:T(8,128)(2,1)} %collective-permute-done), channel_id=1, source_target_pairs={{0,4},{4,8},{8,12},{12,16},{16,20},{20,24},{24,28},{1,5},{5,9},{9,... | collective-permute-start | bytes 1572872 | tf_op jit(solution)/shard_map/ppermute | solution.py:13
  76.3 0.0 all-gather.8.cloned.1.call-update
  76.3 0.0 all-gather.6.cloned.1.call-start
  76.4 0.9 collective-permute-done.1
  77.3 2.6 %pad_maximum_fusion.1 = bf16[1,2,1536,256]{2,3,1,0:T(8,128)(2,1)} fusion(bf16[1,2,512,256]{2,3,1,0:T(8,128)(2,1)} %copy-done.2, bf16[1,2,512,256]{2,3,1,0:T(8,128)(2,1)} %collective-permute-done, bf16[1,2,512,256]{2,3,1,0:T(8,128)(2,1)} %collective-permute-done.1), kind=kLoop, calls=%fused_computation.25 | loop fusion | flops 4718592 | bytes 3145728 | tf_op jit(solution)/shard_map/concatenate | solution.py:67
  80.0 4.9 %copy.23 = bf16[1,2,1536,256]{3,1,2,0:T(2,128)(2,1)} copy(bf16[1,2,1536,256]{2,3,1,0:T(8,128)(2,1)} %pad_maximum_fusion.1) | data formatting | bytes 3145728
  84.9 5.0 %multiply_reduce_fusion = bf16[2,256,512]{1,0,2:T(2,128)(2,1)} fusion(bf16[2,256,3,512]{1,0,2,3:T(2,128)(2,1)} %bitcast.45, f32[2,256,3]{1,0,2:T(2,128)S(1)} %bitcast_convert_fusion), kind=kLoop, calls=%fused_computation.11 | loop fusion | flops 2097152 | bytes 2103296
  89.9 2.0 %copy.20 = bf16[2,256,512]{2,1,0:T(8,128)(2,1)} copy(bf16[2,256,512]{1,0,2:T(2,128)(2,1)} %multiply_reduce_fusion) | data formatting | bytes 1048576 | tf_op jit(solution)/shard_map/bkltc,tkc->bklc/dot_general | solution.py:26
  91.9 11.8 %collective-permute-start.2 = (bf16[1,2,512,256]{2,3,1,0:T(8,128)(2,1)}, bf16[1,2,512,256]{2,3,1,0:T(8,128)(2,1)S(1)}, u32[]{:S(2)}, u32[]{:S(2)}) collective-permute-start(bf16[1,2,512,256]{2,3,1,0:T(8,128)(2,1)} %bitcast.49), channel_id=1, source_target_pairs={{0,8},{4,12},{8,16},{12,20},{16,24},{20,28},{1,9},{5,13},{9,17},{1... | collective-permute-start | bytes 1572872 | tf_op jit(solution)/shard_map/ppermute | solution.py:13
  103.7 1.6 fusion.10
  105.3 1.0 slice.18
  106.3 9.7 %collective-permute-done.2 = bf16[1,2,512,256]{2,3,1,0:T(8,128)(2,1)S(1)} collective-permute-done((bf16[1,2,512,256]{2,3,1,0:T(8,128)(2,1)}, bf16[1,2,512,256]{2,3,1,0:T(8,128)(2,1)S(1)}, u32[]{:S(2)}, u32[]{:S(2)}) %collective-permute-start.2) | collective-permute-done | bytes 524320 | tf_op jit(solution)/shard_map/ppermute | solution.py:13
  116.0 1.3 pad_maximum_fusion
  117.3 1.3 fusion.39
  118.6 3.8 %fusion.40 = f32[2,512]{1,0:T(2,128)S(1)} fusion(pred[512,1536]{1,0:T(8,128)(4,1)} %fusion.10, bf16[512,2,128]{0,2,1:T(8,128)(2,1)S(1)} %bitcast.50, bf16[1536,2,128]{0,2,1:T(8,128)(2,1)} %bitcast.46), kind=kOutput, calls=%fused_computation.53 | convolution fusion | flops 408946176 | bytes 1839104 | tf_op jit(solution)/shard_map/sub | solution.py:52
  122.5 5.2 %fusion.25 = bf16[2,128,512]{2,1,0:T(8,128)(2,1)} fusion(bf16[1536,2,128]{0,2,1:T(8,128)(2,1)} %bitcast.48, f32[2,512]{1,0:T(2,128)S(1)} %fusion.40, pred[512,1536]{1,0:T(8,128)(4,1)} %fusion.10, bf16[512,2,128]{0,2,1:T(8,128)(2,1)S(1)} %bitcast.51, bf16[1536,2,128]{0,2,1:T(8,128)(2,1)} %bitcast.47), kind=kOutput, calls=%fused_computation.32 | convolution fusion | flops 813304320 | bytes 2887680 | tf_op jit(solution)/shard_map/bhqk,bkhd->bqhd/dot_general | solution.py:54
  127.6 0.0 all-gather.6.cloned.1.call-update
  127.7 0.0 all-gather.8.cloned.1.call-done
  127.7 26.1 %all-gather.6.cloned.1.call-done = bf16[1,512,1024]{1,2,0:T(8,128)(2,1)} async-done(((bf16[1,512,256]{1,2,0:T(8,128)(2,1)}), bf16[1,512,1024]{1,2,0:T(8,128)(2,1)}) %all-gather.6.cloned.1.call-update) | async-done | bytes 1048592 | tf_op jit(solution)/shard_map/all_gather | solution.py:72
  153.8 3.1 %fusion.24 = bf16[1,512,512]{2,1,0:T(8,128)(2,1)} fusion(bf16[1024,512]{1,0:T(8,128)(2,1)} %all-gather.8.cloned.1.call-done, bf16[1,512,1024]{1,2,0:T(8,128)(2,1)} %all-gather.6.cloned.1.call-done), kind=kOutput, calls=%fused_computation.31 | convolution fusion | flops 537133056 | bytes 2621440 | tf_op jit(solution)/shard_map/blr,rc->blc/dot_general | solution.py:74
  (14 shorter events, 0.1 us)
Async XLA Ops:
  7.4 53.7 %copy-start = (bf16[2048,3,256]{2,0,1:T(8,128)(2,1)S(1)}, bf16[2048,3,256]{2,0,1:T(8,128)(2,1)}, u32[]{:S(2)}) copy-start(bf16[2048,3,256]{2,0,1:T(8,128)(2,1)} %param.5) | copy-start | bytes 9437188
  7.4 50.8 %all-gather.4.cloned.1.call-start = ((), (), s32[]{:S(2)}) async-start(), calls=%async_computation | async-start | bytes 2621440 | tf_op jit(solution)/shard_map/all_gather | solution.py:59
  8.1 119.6 %all-gather.8.cloned.1.call-start = ((), (), s32[]{:S(2)}) async-start(), calls=%async_computation.2 | async-start | bytes 1179648 | tf_op jit(solution)/shard_map/all_gather | solution.py:73
  58.1 2.2 %copy-start.1 = (bf16[1,512,2048]{2,1,0:T(8,128)(2,1)S(1)}, bf16[1,512,2048]{2,1,0:T(8,128)(2,1)}, u32[]{:S(2)}) copy-start(bf16[1,512,2048]{2,1,0:T(8,128)(2,1)} %all-gather.4.cloned.1.call-done) | copy-start | bytes 6291460
  61.1 15.3 %copy-start.4 = (bf16[3,2,256]{2,1,0:T(2,128)(2,1)S(1)}, bf16[3,2,256]{2,1,0:T(2,128)(2,1)}, u32[]{:S(2)}) copy-start(bf16[3,2,256]{2,1,0:T(2,128)(2,1)} %param.6) | copy-start | bytes 9220
  63.1 4.1 %copy-start.3 = (bf16[1,3,512,256]{2,3,1,0:T(8,128)(2,1)}, bf16[1,3,512,256]{2,3,1,0:T(8,128)(2,1)S(1)}, u32[]{:S(2)}) copy-start(bf16[1,3,512,256]{2,3,1,0:T(8,128)(2,1)S(1)} %fusion.21) | copy-start | bytes 2359300
  63.1 0.9 copy-start.2
  64.0 3.2 %collective-permute-start = (bf16[1,2,512,256]{2,3,1,0:T(8,128)(2,1)S(1)}, bf16[1,2,512,256]{2,3,1,0:T(8,128)(2,1)}, u32[]{:S(2)}, u32[]{:S(2)}) collective-permute-start(bf16[1,2,512,256]{2,3,1,0:T(8,128)(2,1)S(1)} %slice.16), channel_id=1, source_target_pairs={{0,4},{4,8},{8,12},{12,16},{16,20},{20,24},{24,28},{1,5},{5,9},{9,... | collective-permute-start | bytes 1572872 | tf_op jit(solution)/shard_map/ppermute | solution.py:13
  67.2 10.1 %collective-permute-start.1 = (bf16[1,2,512,256]{2,3,1,0:T(8,128)(2,1)}, bf16[1,2,512,256]{2,3,1,0:T(8,128)(2,1)}, u32[]{:S(2)}, u32[]{:S(2)}) collective-permute-start(bf16[1,2,512,256]{2,3,1,0:T(8,128)(2,1)} %collective-permute-done), channel_id=1, source_target_pairs={{0,4},{4,8},{8,12},{12,16},{16,20},{20,24},{24,28},{1,5},{5,9},{9,... | collective-permute-start | bytes 1572872 | tf_op jit(solution)/shard_map/ppermute | solution.py:13
  76.3 77.5 %all-gather.6.cloned.1.call-start = ((), (), s32[]{:S(2)}) async-start(), calls=%async_computation.1 | async-start | bytes 1310720 | tf_op jit(solution)/shard_map/all_gather | solution.py:72
  91.9 24.1 %collective-permute-start.2 = (bf16[1,2,512,256]{2,3,1,0:T(8,128)(2,1)}, bf16[1,2,512,256]{2,3,1,0:T(8,128)(2,1)S(1)}, u32[]{:S(2)}, u32[]{:S(2)}) collective-permute-start(bf16[1,2,512,256]{2,3,1,0:T(8,128)(2,1)} %bitcast.49), channel_id=1, source_target_pairs={{0,8},{4,12},{8,16},{12,20},{16,24},{20,28},{1,9},{5,13},{9,17},{1... | collective-permute-start | bytes 1572872 | tf_op jit(solution)/shard_map/ppermute | solution.py:13
Sparse Core Ops, SparseCore 0:
  9.7 48.3 all-gather.3
Sparse Core Ops, SparseCore 1:
  76.4 23.4 all-gather.7
  127.7 26.0 all-gather.5
where the time goes:
time: 165 us; the launch traced here: 164 us
  waiting for transfers between devices  88.4 us (54%)
  starting transfers between devices  23.3 us (14%)
  between operations  15 us (9%)
  matrix products  14.1 us (9%)
  other arithmetic  13.4 us (8%)
  local copies, waits for them, and re-layouts  10.2 us (6%)
    all_gather x1, waiting for transfers between devices, local(): gathered = lax.all_gather(layer_input, 'head', axis=2, tiled=True)  50 us
    all_gather x1, waiting for transfers between devices, local(): full_ctx = lax.all_gather(context, 'head', axis=2, tiled=True)  26.1 us
    ppermute x3, starting transfers between devices, passed_along(): return lax.ppermute(block, axis, route)  23.2 us
    ppermute x3, waiting for transfers between devices, passed_along(): return lax.ppermute(block, axis, route)  11.5 us
    unnamed x11, local copies, waits for them, and re-layouts  5.9 us
    dot_general x1, matrix products, attend(): jnp.einsum('bhqk,bkhd->bqhd', weights, value_heads, preferred_element_typ...  5.18 us
    unnamed x2, other arithmetic  5.02 us
    sub x1, matrix products, attend(): exponent = jnp.exp(scores - highest)  3.83 us
  transfers between devices with their start and end apart: 6, of which 5 were waited for; matrix products, arithmetic and copies ran while one was open for 18% of the time, Pallas kernels for 0%

commit v1 on v0

--- a/solution.py
+++ b/solution.py
@@ -56,7 +56,26 @@
 
 
 def local(layer_input, w_qkv, comp_weight, w_out):
-    gathered = lax.all_gather(layer_input, "head", axis=2, tiled=True)
+    size, position, rows = (lax.axis_size("head"), lax.axis_index("head"), layer_input.shape[2])
+    upward = [(i_2, (i_2 + 1) % size) for i_2 in range(size)]
+    backward = [(i_2, (i_2 - 1) % size) for i_2 in range(size)]
+    out = jnp.zeros(
+        (*layer_input.shape[:2], size * rows, *layer_input.shape[2 + 1 :]), layer_input.dtype
+    )
+    out = lax.dynamic_update_slice_in_dim(out, layer_input, position * rows, axis=2)
+    from_left = from_right = layer_input
+    halfway = size // 2
+    for hop in range(1, halfway + 1):
+        from_left = lax.ppermute(from_left, "head", upward)
+        out = lax.dynamic_update_slice_in_dim(
+            out, from_left, (position - hop) % size * rows, axis=2
+        )
+        if hop < size - halfway:
+            from_right = lax.ppermute(from_right, "head", backward)
+            out = lax.dynamic_update_slice_in_dim(
+                out, from_right, (position + hop) % size * rows, axis=2
+            )
+    gathered = out
     normed = layer_norm(gathered.astype(jnp.float32)).astype(jnp.bfloat16)
     projected = jnp.einsum("bld,dkc->bklc", normed, w_qkv, preferred_element_type=jnp.float32)
     projected = projected.astype(jnp.bfloat16)

time: 165 us -> 152 us (0.921)
  waiting for transfers between devices: 88.4 us -> 69.2 us
  starting transfers between devices: 23.3 us -> 28.2 us
  local copies, waits for them, and re-layouts: 10.2 us -> 14.7 us
  other arithmetic: 13.4 us -> 11.7 us
    all_gather x1 -> x0, waiting for transfers between devices: 50 us -> none  [local(): gathered = lax.all_gather(layer_input, 'head', axis=2, tiled=True)]
    ppermute x0 -> x3, waiting for transfers between devices: none -> 31.1 us  [the longest x2 23.6 us: local(): from_left = lax.ppermute(from_left, 'head', upward)]
    ppermute x0 -> x3, starting transfers between devices: none -> 5.08 us  [the longest x2 3.05 us: local(): from_left = lax.ppermute(from_left, 'head', upward)]
    dynamic_update_slice x0 -> x4, local copies, waits for them, and re-layouts: none -> 4.42 us  [the longest x2 2.21 us: local(): lax.dynamic_update_slice_in_dim(out, from_left, (position - hop) % size *...]
    reduce_sum x1, other arithmetic: 2.09 us -> 0.35 us  [layer_norm(): center_mean = jnp.mean(values, axis=-1, keepdims=True)]
    unnamed x11 -> x9, local copies, waits for them, and re-layouts: 5.9 us -> 5.79 us
  transfers between devices with their start and end apart: 6 -> 8, of which waited for: 5 -> 7; matrix products, arithmetic and copies ran while one was open for 18% -> 21% of each run, Pallas kernels for 0% -> 0%
where the time goes in v1:
time: 152 us; the launch traced here: 151 us
  waiting for transfers between devices  69.2 us (46%)
  starting transfers between devices  28.2 us (19%)
  local copies, waits for them, and re-layouts  14.7 us (10%)
  matrix products  14.1 us (9%)
  between operations  13.6 us (9%)
  other arithmetic  11.7 us (8%)
    all_gather x1, waiting for transfers between devices, local(): full_ctx = lax.all_gather(context, 'head', axis=2, tiled=True)  27.4 us
    ppermute x2, waiting for transfers between devices, local(): from_left = lax.ppermute(from_left, 'head', upward)  23.6 us
    ppermute x3, starting transfers between devices, passed_along(): return lax.ppermute(block, axis, route)  23.1 us
    ppermute x3, waiting for transfers between devices, passed_along(): return lax.ppermute(block, axis, route)  10.6 us
    ppermute x1, waiting for transfers between devices, local(): from_right = lax.ppermute(from_right, 'head', backward)  7.53 us
    unnamed x9, local copies, waits for them, and re-layouts  5.79 us
    dot_general x1, matrix products, attend(): jnp.einsum('bhqk,bkhd->bqhd', weights, value_heads, preferred_element_typ...  5.18 us
    unnamed x2, other arithmetic  5.02 us
  transfers between devices with their start and end apart: 8, of which 7 were waited for; matrix products, arithmetic and copies ran while one was open for 21% of the time, Pallas kernels for 0%

profile of v1, /device:TPU:0, one launch (start us, length us, event | category | flops | bytes accessed | tf_op | source)
XLA Modules:
  0.0 151.5 jit_solution(6892430583196126167)
XLA Ops:
  6.5 3.1 %collective-permute-start = (bf16[1,512,512]{2,1,0:T(8,128)(2,1)}, bf16[1,512,512]{2,1,0:T(8,128)(2,1)}, u32[]{:S(2)}, u32[]{:S(2)}) collective-permute-start(bf16[1,512,512]{2,1,0:T(8,128)(2,1)} %param.4), channel_id=1, source_target_pairs={{0,1},{1,2},{2,3},{3,0},{4,5},{5,6},{6,7},{7,4},{8,9},{9,10},{10,1... | collective-permute-start | bytes 1572872 | tf_op jit(solution)/shard_map/ppermute | solution.py:69
  9.6 2.0 %collective-permute-start.1 = (bf16[1,512,512]{2,1,0:T(8,128)(2,1)}, bf16[1,512,512]{2,1,0:T(8,128)(2,1)}, u32[]{:S(2)}, u32[]{:S(2)}) collective-permute-start(bf16[1,512,512]{2,1,0:T(8,128)(2,1)} %param.4), channel_id=1, source_target_pairs={{0,3},{1,0},{2,1},{3,2},{4,7},{5,4},{6,5},{7,6},{8,11},{9,8},{10,9... | collective-permute-start | bytes 1572872 | tf_op jit(solution)/shard_map/ppermute | solution.py:74
  11.6 13.1 %collective-permute-done = bf16[1,512,512]{2,1,0:T(8,128)(2,1)} collective-permute-done((bf16[1,512,512]{2,1,0:T(8,128)(2,1)}, bf16[1,512,512]{2,1,0:T(8,128)(2,1)}, u32[]{:S(2)}, u32[]{:S(2)}) %collective-permute-start) | collective-permute-done | bytes 524320 | tf_op jit(solution)/shard_map/ppermute | solution.py:69
  24.8 0.2 broadcast_in_dim.14
  25.0 1.1 constant_dynamic-update-slice_fusion.3
  26.1 1.1 constant_dynamic-update-slice_fusion.2
  27.2 7.5 %collective-permute-done.1 = bf16[1,512,512]{2,1,0:T(8,128)(2,1)} collective-permute-done((bf16[1,512,512]{2,1,0:T(8,128)(2,1)}, bf16[1,512,512]{2,1,0:T(8,128)(2,1)}, u32[]{:S(2)}, u32[]{:S(2)}) %collective-permute-start.1) | collective-permute-done | bytes 524320 | tf_op jit(solution)/shard_map/ppermute | solution.py:74
  34.8 1.1 constant_dynamic-update-slice_fusion.1
  35.9 10.5 %collective-permute-done.2 = bf16[1,512,512]{2,1,0:T(8,128)(2,1)} collective-permute-done((bf16[1,512,512]{2,1,0:T(8,128)(2,1)}, bf16[1,512,512]{2,1,0:T(8,128)(2,1)}, u32[]{:S(2)}, u32[]{:S(2)}) %collective-permute-start.2) | collective-permute-done | bytes 524320 | tf_op jit(solution)/shard_map/ppermute | solution.py:69
  46.4 1.1 constant_dynamic-update-slice_fusion
  47.5 0.4 convert_reduce_fusion
  47.8 0.7 fusion.4
  48.6 2.0 %fusion.21 = bf16[1,3,512,256]{2,3,1,0:T(8,128)(2,1)S(1)} fusion(bf16[2048,3,256]{2,0,1:T(8,128)(2,1)S(1)} %copy-done, bf16[1,512,2048]{2,1,0:T(8,128)(2,1)S(1)} %constant_dynamic-update-slice_fusion, f32[512]{0:T(512)S(1)} %add_rsqrt_fusion, f32[512]{0:T(512)S(1)} %broadcast_multiply_fusion), kind=kOutput, calls=%fused_computation.29 | convolution fusion | flops 1615200256 | bytes 6033408 | tf_op jit(solution)/shard_map/bld,dkc->bklc/dot_general | solution.py:80
  50.6 0.8 copy-done.1
  51.5 2.1 %collective-permute-start.3 = (bf16[1,2,512,256]{2,3,1,0:T(8,128)(2,1)S(1)}, bf16[1,2,512,256]{2,3,1,0:T(8,128)(2,1)}, u32[]{:S(2)}, u32[]{:S(2)}) collective-permute-start(bf16[1,2,512,256]{2,3,1,0:T(8,128)(2,1)S(1)} %slice.16), channel_id=1, source_target_pairs={{0,4},{4,8},{8,12},{12,16},{16,20},{20,24},{24,28},{1,5},{5,9},{9,... | collective-permute-start | bytes 1572872 | tf_op jit(solution)/shard_map/ppermute | solution.py:13
  53.6 0.8 collective-permute-done.3
  54.4 9.4 %collective-permute-start.4 = (bf16[1,2,512,256]{2,3,1,0:T(8,128)(2,1)}, bf16[1,2,512,256]{2,3,1,0:T(8,128)(2,1)}, u32[]{:S(2)}, u32[]{:S(2)}) collective-permute-start(bf16[1,2,512,256]{2,3,1,0:T(8,128)(2,1)} %collective-permute-done.3), channel_id=1, source_target_pairs={{0,4},{4,8},{8,12},{12,16},{16,20},{20,24},{24,28},{1,5},{5,9},{9,... | collective-permute-start | bytes 1572872 | tf_op jit(solution)/shard_map/ppermute | solution.py:13
  63.9 0.9 collective-permute-done.4
  64.8 2.6 %pad_maximum_fusion.1 = bf16[1,2,1536,256]{2,3,1,0:T(8,128)(2,1)} fusion(bf16[1,2,512,256]{2,3,1,0:T(8,128)(2,1)} %copy-done.1, bf16[1,2,512,256]{2,3,1,0:T(8,128)(2,1)} %collective-permute-done.3, bf16[1,2,512,256]{2,3,1,0:T(8,128)(2,1)} %collective-permute-done.4), kind=kLoop, calls=%fused_computation.25 | loop fusion | flops 4718592 | bytes 3145728 | tf_op jit(solution)/shard_map/concatenate | solution.py:86
  67.5 4.9 %copy.23 = bf16[1,2,1536,256]{3,1,2,0:T(2,128)(2,1)} copy(bf16[1,2,1536,256]{2,3,1,0:T(8,128)(2,1)} %pad_maximum_fusion.1) | data formatting | bytes 3145728
  72.4 5.0 %multiply_reduce_fusion = bf16[2,256,512]{1,0,2:T(2,128)(2,1)} fusion(bf16[2,256,3,512]{1,0,2,3:T(2,128)(2,1)} %bitcast.45, f32[2,256,3]{1,0,2:T(2,128)S(1)} %bitcast_convert_fusion), kind=kLoop, calls=%fused_computation.11 | loop fusion | flops 2097152 | bytes 2103296
  77.4 2.0 %copy.20 = bf16[2,256,512]{2,1,0:T(8,128)(2,1)} copy(bf16[2,256,512]{1,0,2:T(2,128)(2,1)} %multiply_reduce_fusion) | data formatting | bytes 1048576 | tf_op jit(solution)/shard_map/bkltc,tkc->bklc/dot_general | solution.py:26
  79.4 11.6 %collective-permute-start.5 = (bf16[1,2,512,256]{2,3,1,0:T(8,128)(2,1)}, bf16[1,2,512,256]{2,3,1,0:T(8,128)(2,1)S(1)}, u32[]{:S(2)}, u32[]{:S(2)}) collective-permute-start(bf16[1,2,512,256]{2,3,1,0:T(8,128)(2,1)} %bitcast.49), channel_id=1, source_target_pairs={{0,8},{4,12},{8,16},{12,20},{16,24},{20,28},{1,9},{5,13},{9,17},{1... | collective-permute-start | bytes 1572872 | tf_op jit(solution)/shard_map/ppermute | solution.py:13
  91.1 1.6 %fusion.10 = pred[512,1536]{1,0:T(8,128)(4,1)} fusion(s32[1536]{0:T(1024)S(1)} %iota_add_fusion, pred[1536]{0:T(1024)(128)(4,1)S(1)} %get-tuple-element.8, pred[1536]{0:T(1024)(128)(4,1)S(1)} %fusion.31, pred[1536]{0:T(1024)(128)(4,1)S(1)} %get-tuple-element.7), kind=kLoop, calls=%fused_computation.17 | loop fusion | flops 3145728 | bytes 797184 | tf_op jit(solution)/shard_map/or | solution.py:36
  92.7 1.0 slice.18
  93.7 8.8 %collective-permute-done.5 = bf16[1,2,512,256]{2,3,1,0:T(8,128)(2,1)S(1)} collective-permute-done((bf16[1,2,512,256]{2,3,1,0:T(8,128)(2,1)}, bf16[1,2,512,256]{2,3,1,0:T(8,128)(2,1)S(1)}, u32[]{:S(2)}, u32[]{:S(2)}) %collective-permute-start.5) | collective-permute-done | bytes 524320 | tf_op jit(solution)/shard_map/ppermute | solution.py:13
  102.5 1.3 pad_maximum_fusion
  103.8 1.3 fusion.39
  105.1 3.8 %fusion.40 = f32[2,512]{1,0:T(2,128)S(1)} fusion(pred[512,1536]{1,0:T(8,128)(4,1)} %fusion.10, bf16[512,2,128]{0,2,1:T(8,128)(2,1)S(1)} %bitcast.50, bf16[1536,2,128]{0,2,1:T(8,128)(2,1)} %bitcast.46), kind=kOutput, calls=%fused_computation.57 | convolution fusion | flops 408946176 | bytes 1839104 | tf_op jit(solution)/shard_map/sub | solution.py:52
  108.9 5.2 %fusion.25 = bf16[2,128,512]{2,1,0:T(8,128)(2,1)} fusion(bf16[1536,2,128]{0,2,1:T(8,128)(2,1)} %bitcast.48, f32[2,512]{1,0:T(2,128)S(1)} %fusion.40, pred[512,1536]{1,0:T(8,128)(4,1)} %fusion.10, bf16[512,2,128]{0,2,1:T(8,128)(2,1)S(1)} %bitcast.51, bf16[1536,2,128]{0,2,1:T(8,128)(2,1)} %bitcast.47), kind=kOutput, calls=%fused_computation.32 | convolution fusion | flops 813304320 | bytes 2887680 | tf_op jit(solution)/shard_map/bhqk,bkhd->bqhd/dot_general | solution.py:54
  114.2 27.4 %all-gather.3.cloned.1.call-done = bf16[1,512,1024]{1,2,0:T(8,128)(2,1)} async-done(((bf16[1,512,256]{1,2,0:T(8,128)(2,1)}), bf16[1,512,1024]{1,2,0:T(8,128)(2,1)}) %all-gather.3.cloned.1.call-update) | async-done | bytes 1048592 | tf_op jit(solution)/shard_map/all_gather | solution.py:91
  141.6 3.1 %fusion.24 = bf16[1,512,512]{2,1,0:T(8,128)(2,1)} fusion(bf16[1024,512]{1,0:T(8,128)(2,1)} %all-gather.5.cloned.1.call-done, bf16[1,512,1024]{1,2,0:T(8,128)(2,1)} %all-gather.3.cloned.1.call-done), kind=kOutput, calls=%fused_computation.31 | convolution fusion | flops 537133056 | bytes 2621440 | tf_op jit(solution)/shard_map/blr,rc->blc/dot_general | solution.py:93
  (20 shorter events, 0.2 us)
Async XLA Ops:
  6.5 42.0 %copy-start = (bf16[2048,3,256]{2,0,1:T(8,128)(2,1)S(1)}, bf16[2048,3,256]{2,0,1:T(8,128)(2,1)}, u32[]{:S(2)}) copy-start(bf16[2048,3,256]{2,0,1:T(8,128)(2,1)} %param.5) | copy-start | bytes 9437188
  6.5 107.6 %all-gather.5.cloned.1.call-start = ((), (), s32[]{:S(2)}) async-start(), calls=%async_computation.1 | async-start | bytes 1179648 | tf_op jit(solution)/shard_map/all_gather | solution.py:92
  6.5 18.2 %collective-permute-start = (bf16[1,512,512]{2,1,0:T(8,128)(2,1)}, bf16[1,512,512]{2,1,0:T(8,128)(2,1)}, u32[]{:S(2)}, u32[]{:S(2)}) collective-permute-start(bf16[1,512,512]{2,1,0:T(8,128)(2,1)} %param.4), channel_id=1, source_target_pairs={{0,1},{1,2},{2,3},{3,0},{4,5},{5,6},{6,7},{7,4},{8,9},{9,10},{10,1... | collective-permute-start | bytes 1572872 | tf_op jit(solution)/shard_map/ppermute | solution.py:69
  9.6 25.2 %collective-permute-start.1 = (bf16[1,512,512]{2,1,0:T(8,128)(2,1)}, bf16[1,512,512]{2,1,0:T(8,128)(2,1)}, u32[]{:S(2)}, u32[]{:S(2)}) collective-permute-start(bf16[1,512,512]{2,1,0:T(8,128)(2,1)} %param.4), channel_id=1, source_target_pairs={{0,3},{1,0},{2,1},{3,2},{4,7},{5,4},{6,5},{7,6},{8,11},{9,8},{10,9... | collective-permute-start | bytes 1572872 | tf_op jit(solution)/shard_map/ppermute | solution.py:74
  24.8 21.6 %collective-permute-start.2 = (bf16[1,512,512]{2,1,0:T(8,128)(2,1)}, bf16[1,512,512]{2,1,0:T(8,128)(2,1)}, u32[]{:S(2)}, u32[]{:S(2)}) collective-permute-start(bf16[1,512,512]{2,1,0:T(8,128)(2,1)} %collective-permute-done), channel_id=1, source_target_pairs={{0,1},{1,2},{2,3},{3,0},{4,5},{5,6},{6,7},{7,4},{8,9},{9,10},{10,1... | collective-permute-start | bytes 1572872 | tf_op jit(solution)/shard_map/ppermute | solution.py:69
  48.6 15.3 %copy-start.3 = (bf16[3,2,256]{2,1,0:T(2,128)(2,1)S(1)}, bf16[3,2,256]{2,1,0:T(2,128)(2,1)}, u32[]{:S(2)}) copy-start(bf16[3,2,256]{2,1,0:T(2,128)(2,1)} %param.6) | copy-start | bytes 9220
  50.6 3.8 %copy-start.2 = (bf16[1,3,512,256]{2,3,1,0:T(8,128)(2,1)}, bf16[1,3,512,256]{2,3,1,0:T(8,128)(2,1)S(1)}, u32[]{:S(2)}) copy-start(bf16[1,3,512,256]{2,3,1,0:T(8,128)(2,1)S(1)} %fusion.21) | copy-start | bytes 2359300
  50.6 0.8 copy-start.1
  51.5 2.9 %collective-permute-start.3 = (bf16[1,2,512,256]{2,3,1,0:T(8,128)(2,1)S(1)}, bf16[1,2,512,256]{2,3,1,0:T(8,128)(2,1)}, u32[]{:S(2)}, u32[]{:S(2)}) collective-permute-start(bf16[1,2,512,256]{2,3,1,0:T(8,128)(2,1)S(1)} %slice.16), channel_id=1, source_target_pairs={{0,4},{4,8},{8,12},{12,16},{16,20},{20,24},{24,28},{1,5},{5,9},{9,... | collective-permute-start | bytes 1572872 | tf_op jit(solution)/shard_map/ppermute | solution.py:13
  54.4 10.4 %collective-permute-start.4 = (bf16[1,2,512,256]{2,3,1,0:T(8,128)(2,1)}, bf16[1,2,512,256]{2,3,1,0:T(8,128)(2,1)}, u32[]{:S(2)}, u32[]{:S(2)}) collective-permute-start(bf16[1,2,512,256]{2,3,1,0:T(8,128)(2,1)} %collective-permute-done.3), channel_id=1, source_target_pairs={{0,4},{4,8},{8,12},{12,16},{16,20},{20,24},{24,28},{1,5},{5,9},{9,... | collective-permute-start | bytes 1572872 | tf_op jit(solution)/shard_map/ppermute | solution.py:13
  63.8 77.8 %all-gather.3.cloned.1.call-start = ((), (), s32[]{:S(2)}) async-start(), calls=%async_computation | async-start | bytes 1310720 | tf_op jit(solution)/shard_map/all_gather | solution.py:91
  79.4 23.1 %collective-permute-start.5 = (bf16[1,2,512,256]{2,3,1,0:T(8,128)(2,1)}, bf16[1,2,512,256]{2,3,1,0:T(8,128)(2,1)S(1)}, u32[]{:S(2)}, u32[]{:S(2)}) collective-permute-start(bf16[1,2,512,256]{2,3,1,0:T(8,128)(2,1)} %bitcast.49), channel_id=1, source_target_pairs={{0,8},{4,12},{8,16},{12,20},{16,24},{20,28},{1,9},{5,13},{9,17},{1... | collective-permute-start | bytes 1572872 | tf_op jit(solution)/shard_map/ppermute | solution.py:13
Sparse Core Ops, SparseCore 0:
  63.9 24.0 all-gather.4
  114.2 27.2 all-gather.2
